TPU v7x, 256 devices: a whole 4x4x8 slice. The times are simulated.
256 devices in a mesh: blk: 32 (over x_lo, z, core), head: 8 (over y, x_hi).
Axes of the slice: x: 4 (x_hi: 2, x_lo: 2; x = x_hi * 2 + x_lo), y: 4, z: 8, core: 2. Of those that a mesh axis runs over, the one named last changes fastest.
Arguments:
- queries: bfloat16 [2, 4096, 32, 128], P(None, 'blk', 'head'), may hold values from -30 to 30
- new_keys: bfloat16 [2, 4096, 16, 128], P(None, 'blk', 'head'), may hold values from -30 to 30
- new_values: bfloat16 [2, 4096, 16, 128], P(None, 'blk', 'head'), may hold values from -6 to 6
- pool_keys: bfloat16 [64, 128, 16, 128], P('blk', None, 'head'), may hold values from -30 to 30
- pool_values: bfloat16 [64, 128, 16, 128], P('blk', None, 'head'), may hold values from -6 to 6
- page_table: int32 [2, 32], replicated, may hold values from 0 to 63, as said below
- cache_len: int32 [2], replicated, may hold values from 1024 to 4096, as said below
- out_weight: bfloat16 [32, 128, 4608], P('head'), may hold values from -0.09375 to 0.09375
- residual: bfloat16 [2, 4096, 4608], P(None, ('blk', 'head')), may hold values from -6 to 6
- post_gain: float32 [4608], replicated, may hold values from 0.1 to 1.9
Outputs:
- mixed: bfloat16 [2, 4096, 4608], P(None, ('blk', 'head'))
Inputs may be any that keep to these rules, and one draw needn't show every extreme that they name: `page_table`: every pool page appears exactly once in the table. `cache_len`: one request has exactly 4096 cached tokens.
All inputs are finite; a program needn't handle non-finite values.
Results may differ from a plain program's by a relative error of at most 0.015.
Values may be sent and summed in bfloat16 or wider, within the bound.
A program may use at most 128 MiB of HBM per device.

v0:
```python
import jax
import jax.numpy as jnp
from jax import lax
from jax.sharding import PartitionSpec as P

soft_cap = 50.0
score_scale = 144.0 ** (-0.5)
norm_eps = 1e-06


def group_pages(page_count, page_len):
    width = max(1, min(page_count, 2048 // page_len))
    while page_count % width:
        width -= 1
    return width


def attend_pages(running, grouped, key_pages, value_pages, valid_keys):
    page_count, page_len, kv_heads, head_dim = key_pages.shape
    tok_rows = valid_keys.shape[1]
    width = group_pages(page_count, page_len)
    groups = page_count // width
    key_groups = key_pages.reshape(groups, width * page_len, kv_heads, head_dim)
    value_groups = value_pages.reshape(groups, width * page_len, kv_heads, head_dim)
    valid_groups = (
        valid_keys.reshape(groups, width, tok_rows, page_len)
        .transpose(0, 2, 1, 3)
        .reshape(groups, tok_rows, width * page_len)
    )

    def compute(carry_in, key_block, value_block, valid_block):
        numerator, denominator = carry_in
        scores = (
            jnp.einsum("tkgd,skd->kgts", grouped, key_block, preferred_element_type=jnp.float32)
            * score_scale
        )
        capped = soft_cap * jnp.tanh(scores / soft_cap)
        weights = jnp.where(valid_block[None, None], jnp.exp(capped), 0.0).astype(jnp.bfloat16)
        numerator = numerator + jnp.einsum(
            "kgts,skd->tkgd", weights, value_block, preferred_element_type=jnp.float32
        )
        denominator = denominator + jnp.sum(weights.astype(jnp.float32), axis=-1)
        return (numerator, denominator)

    def one_group(carry_in, inputs):
        key_block, value_block, valid_block = inputs
        carry_out = compute(carry_in, key_block, value_block, valid_block)
        return (carry_out, None)

    result, _ = lax.scan(one_group, running, (key_groups, value_groups, valid_groups))
    return result


def shards(
    queries,
    new_keys,
    new_values,
    pool_keys,
    pool_values,
    page_table,
    cache_len,
    out_weight,
    residual,
    post_gain,
):
    req_count, per_req, heads_here, head_dim = queries.shape
    tok_dev = req_count * per_req
    kv_here = new_keys.shape[2]
    page_len = pool_keys.shape[1]
    slot_count = page_table.shape[1]
    blk_place = lax.axis_index("blk")
    row_ids = jnp.arange(tok_dev, dtype=jnp.int32)
    row_request = row_ids // per_req
    row_offset = blk_place * per_req + row_ids % per_req
    grouped = queries.reshape(tok_dev, kv_here, heads_here // kv_here, head_dim)
    page_rows = jnp.arange(page_len, dtype=jnp.int32)
    request_ids = jnp.arange(req_count, dtype=jnp.int32)
    row_onehot = row_request[:, None] == request_ids[None, :]
    start_carry = (
        jnp.zeros((tok_dev, kv_here, heads_here // kv_here, head_dim), jnp.float32),
        jnp.zeros((kv_here, heads_here // kv_here, tok_dev), jnp.float32),
    )
    pieces = (
        lax.all_gather(pool_keys, "blk", axis=0, tiled=True),
        lax.all_gather(pool_values, "blk", axis=0, tiled=True),
    )
    page_ids = jnp.arange(pieces[0].shape[0], dtype=jnp.int32)
    matches = page_ids[:, None, None] == page_table[None, :, :]
    slot_index = jnp.sum(
        jnp.where(matches, jnp.arange(slot_count, dtype=jnp.int32)[None, None, :], 0), axis=2
    )
    owned_page = jnp.any(matches, axis=2)
    position = slot_index[:, :, None] * page_len + page_rows[None, None, :]
    keep_keys = owned_page[:, :, None] & (position < cache_len[None, :, None])
    running = attend_pages(
        start_carry,
        grouped,
        pieces[0],
        pieces[1],
        jnp.any(keep_keys[:, None, :, :] & row_onehot[None, :, :, None], axis=2),
    )
    pieces = (
        lax.all_gather(new_keys, "blk", axis=1, tiled=True),
        lax.all_gather(new_values, "blk", axis=1, tiled=True),
    )
    piece_pages = pieces[0].shape[1] // page_len
    page_index = jnp.arange(req_count * piece_pages, dtype=jnp.int32)
    firsts = page_index % piece_pages * page_len
    key_pages = pieces[0].reshape(req_count * piece_pages, page_len, kv_here, head_dim)
    value_pages = pieces[1].reshape(req_count * piece_pages, page_len, kv_here, head_dim)
    offsets = firsts[:, None] + page_rows[None, :]
    same_request = (page_index // piece_pages)[:, None] == row_request[None, :]
    running = attend_pages(
        running,
        grouped,
        key_pages,
        value_pages,
        same_request[:, :, None] & (offsets[:, None, :] <= row_offset[None, :, None]),
    )
    numerator, denominator = running
    attended = (numerator / jnp.transpose(denominator, (2, 0, 1))[..., None]).astype(jnp.bfloat16)
    head_count = lax.axis_size("head")
    share = per_req // head_count
    feature_len = heads_here * head_dim
    attended = (
        attended.reshape(req_count, head_count, share, feature_len)
        .transpose(1, 0, 2, 3)
        .reshape(tok_dev, feature_len)
    )
    weight_rows = out_weight.reshape(feature_len, out_weight.shape[2])
    projected = lax.psum_scatter(
        jnp.dot(attended, weight_rows, preferred_element_type=jnp.float32).astype(jnp.bfloat16),
        "head",
        scatter_dimension=0,
        tiled=True,
    ).astype(jnp.float32)
    projected = projected.reshape(req_count, share, projected.shape[1])
    inv_rms = lax.rsqrt(jnp.mean(projected * projected, axis=-1, keepdims=True) + norm_eps)
    mixed_out = residual.astype(jnp.float32) + post_gain * projected * inv_rms
    return mixed_out.astype(jnp.bfloat16)


def solution(mesh):
    placed = (
        P(None, "blk", "head", None),
        P(None, "blk", "head", None),
        P(None, "blk", "head", None),
        P("blk", None, "head", None),
        P("blk", None, "head", None),
        P(),
        P(),
        P("head", None, None),
        P(None, ("blk", "head"), None),
        P(),
    )
    return jax.shard_map(
        shards,
        mesh=mesh,
        in_specs=placed,
        out_specs=P(None, ("blk", "head"), None),
        check_vma=False,
    )
```

profile of v0, /device:TPU:32, one launch (start us, length us, event | category | flops | bytes accessed | tf_op | source)
XLA Modules:
  0.0 406.5 jit_solution(9550354351666353231)
XLA Ops:
  6.5 1.6 copy.33
  8.2 1.6 copy.29
  9.9 1.6 copy.37
  11.5 1.6 copy.38
  15.9 3.5 and_reduce_fusion
  19.4 4.8 %copy.32 = pred[4,256,16,128]{1,3,2,0:T(8,128)(4,1)} copy(pred[4,256,16,128]{3,1,2,0:T(8,128)(4,1)S(1)} %bitcast.108) | data formatting | bytes 4194304 | tf_op jit(solution)/shard_map/transpose | solution.py:27
  24.5 1.7 bitcast_and_fusion
  26.2 51.5 %all-gather.7.cloned.1.call-done = bf16[64,128,2,128]{3,1,0,2:T(8,128)(2,1)} async-done(((bf16[2,128,2,128]{3,1,0,2:T(8,128)(2,1)}), bf16[64,128,2,128]{3,1,0,2:T(8,128)(2,1)}) %all-gather.7.cloned.1.call-update) | async-done | bytes 4194320 | tf_op jit(solution)/shard_map/all_gather | solution.py:84
  77.7 68.5 %all-gather.5.cloned.1.call-done = bf16[64,128,2,128]{3,1,0,2:T(8,128)(2,1)} async-done(((bf16[2,128,2,128]{3,1,0,2:T(8,128)(2,1)}), bf16[64,128,2,128]{3,1,0,2:T(8,128)(2,1)}) %all-gather.5.cloned.1.call-update) | async-done | bytes 4194320 | tf_op jit(solution)/shard_map/all_gather | solution.py:85
  146.3 41.6 %while.30 = (s32[]{:T(128)}, f32[256,2,2,128]{0,3,2,1:T(8,128)S(1)}, f32[2,2,256]{2,1,0:T(2,128)S(1)}, bf16[4,2048,2,128]{3,1,0,2:T(8,128)(2,1)}, pred[4,256,204...) while((s32[]{:T(128)}, ...), condition=%wide.region_5.6_spmd.clone, body=%wide.region_3.5_spmd.clone.sunk | while | flops 1086587904 | bytes 13386860 | solution.py:50
  147.5 5.7 %convert_reduce_fusion.5 = (f32[2,2,256]{2,1,0:T(2,128)S(1)}, bf16[2,2,256,2048]{2,3,1,0:T(8,128)(2,1)}) fusion(bf16[256,2,2,128]{3,0,2,1:T(8,128)(2,1)S(1)} %get-tuple-element.391, bf16[4,2048,2,128]{3,1,0,2:T(8,128)(2,1)} %get-tuple-element.390, s32[]{:T(128)} %get-tuple-element.376, pred[256,2048]{0,1:T(8,128)(4,1)S(1)} %dynamic-slice_bitcast_fusion.5), kind=kOutput, calls=%fused_computation.14.clone.1 | convolution fusion | flops 549452800 | bytes 6033920 | tf_op jit(solution)/shard_map/while/body/eval_jaxpr/tkgd,skd->kgts/dot_general | solution.py:34
  153.2 3.4 fusion.47
  157.9 5.7 %convert_reduce_fusion.5 = (f32[2,2,256]{2,1,0:T(2,128)S(1)}, bf16[2,2,256,2048]{2,3,1,0:T(8,128)(2,1)}) fusion(bf16[256,2,2,128]{3,0,2,1:T(8,128)(2,1)S(1)} %get-tuple-element.391, bf16[4,2048,2,128]{3,1,0,2:T(8,128)(2,1)} %get-tuple-element.390, s32[]{:T(128)} %get-tuple-element.376, pred[256,2048]{0,1:T(8,128)(4,1)S(1)} %dynamic-slice_bitcast_fusion.5), kind=kOutput, calls=%fused_computation.14.clone.1 | convolution fusion | flops 549452800 | bytes 6033920 | tf_op jit(solution)/shard_map/while/body/eval_jaxpr/tkgd,skd->kgts/dot_general | solution.py:34
  163.5 3.5 fusion.47
  168.3 5.7 %convert_reduce_fusion.5 = (f32[2,2,256]{2,1,0:T(2,128)S(1)}, bf16[2,2,256,2048]{2,3,1,0:T(8,128)(2,1)}) fusion(bf16[256,2,2,128]{3,0,2,1:T(8,128)(2,1)S(1)} %get-tuple-element.391, bf16[4,2048,2,128]{3,1,0,2:T(8,128)(2,1)} %get-tuple-element.390, s32[]{:T(128)} %get-tuple-element.376, pred[256,2048]{0,1:T(8,128)(4,1)S(1)} %dynamic-slice_bitcast_fusion.5), kind=kOutput, calls=%fused_computation.14.clone.1 | convolution fusion | flops 549452800 | bytes 6033920 | tf_op jit(solution)/shard_map/while/body/eval_jaxpr/tkgd,skd->kgts/dot_general | solution.py:34
  173.9 3.5 fusion.47
  178.7 5.7 %convert_reduce_fusion.5 = (f32[2,2,256]{2,1,0:T(2,128)S(1)}, bf16[2,2,256,2048]{2,3,1,0:T(8,128)(2,1)}) fusion(bf16[256,2,2,128]{3,0,2,1:T(8,128)(2,1)S(1)} %get-tuple-element.391, bf16[4,2048,2,128]{3,1,0,2:T(8,128)(2,1)} %get-tuple-element.390, s32[]{:T(128)} %get-tuple-element.376, pred[256,2048]{0,1:T(8,128)(4,1)S(1)} %dynamic-slice_bitcast_fusion.5), kind=kOutput, calls=%fused_computation.14.clone.1 | convolution fusion | flops 549452800 | bytes 6033920 | tf_op jit(solution)/shard_map/while/body/eval_jaxpr/tkgd,skd->kgts/dot_general | solution.py:34
  184.4 3.5 fusion.47
  187.9 26.7 %all-gather.9.cloned.1.call-done = bf16[2,4096,2,128]{3,1,0,2:T(8,128)(2,1)} async-done(((bf16[2,128,2,128]{3,1,0,2:T(8,128)(2,1)}), bf16[2,4096,2,128]{3,1,0,2:T(8,128)(2,1)}) %all-gather.9.cloned.1.call-update) | async-done | bytes 4194320 | tf_op jit(solution)/shard_map/all_gather | solution.py:104
  214.6 68.1 %all-gather.11.cloned.1.call-done = bf16[2,4096,2,128]{3,1,0,2:T(8,128)(2,1)} async-done(((bf16[2,128,2,128]{3,1,0,2:T(8,128)(2,1)}), bf16[2,4096,2,128]{3,1,0,2:T(8,128)(2,1)}) %all-gather.11.cloned.1.call-update) | async-done | bytes 4194320 | tf_op jit(solution)/shard_map/all_gather | solution.py:103
  282.7 26.7 %while.29 = (s32[]{:T(128)}, f32[256,2,2,128]{0,3,2,1:T(8,128)S(1)}, f32[2,2,256]{2,1,0:T(2,128)S(1)}, bf16[4,2048,2,128]{3,1,0,2:T(8,128)(2,1)}, pred[4,256,204...) while((s32[]{:T(128)}, ...), condition=%wide.region_8.9_spmd, body=%wide.region_6.8_spmd.sunk | while | flops 1086455808 | bytes 13386841 | solution.py:50
  282.9 4.3 %convert_reduce_fusion.4 = (f32[2,2,256]{2,1,0:T(2,128)S(1)}, bf16[2,2,256,2048]{2,3,1,0:T(8,128)(2,1)S(1)}) fusion(bf16[256,2,2,128]{3,0,2,1:T(8,128)(2,1)S(1)} %get-tuple-element.416, bf16[4,2048,2,128]{3,1,0,2:T(8,128)(2,1)} %get-tuple-element.415, s32[]{:T(128)} %get-tuple-element.402, pred[256,2048]{0,1:T(8,128)(4,1)S(1)} %dynamic-slice_bitcast_fusion.4), kind=kOutput, calls=%fused_computation.2.clone.1 | convolution fusion | flops 549452800 | bytes 6033920 | tf_op jit(solution)/shard_map/while/body/eval_jaxpr/tkgd,skd->kgts/dot_general | solution.py:34
  287.2 2.1 fusion.43
  289.5 4.3 %convert_reduce_fusion.4 = (f32[2,2,256]{2,1,0:T(2,128)S(1)}, bf16[2,2,256,2048]{2,3,1,0:T(8,128)(2,1)S(1)}) fusion(bf16[256,2,2,128]{3,0,2,1:T(8,128)(2,1)S(1)} %get-tuple-element.416, bf16[4,2048,2,128]{3,1,0,2:T(8,128)(2,1)} %get-tuple-element.415, s32[]{:T(128)} %get-tuple-element.402, pred[256,2048]{0,1:T(8,128)(4,1)S(1)} %dynamic-slice_bitcast_fusion.4), kind=kOutput, calls=%fused_computation.2.clone.1 | convolution fusion | flops 549452800 | bytes 6033920 | tf_op jit(solution)/shard_map/while/body/eval_jaxpr/tkgd,skd->kgts/dot_general | solution.py:34
  293.9 2.1 fusion.43
  296.2 4.3 %convert_reduce_fusion.4 = (f32[2,2,256]{2,1,0:T(2,128)S(1)}, bf16[2,2,256,2048]{2,3,1,0:T(8,128)(2,1)S(1)}) fusion(bf16[256,2,2,128]{3,0,2,1:T(8,128)(2,1)S(1)} %get-tuple-element.416, bf16[4,2048,2,128]{3,1,0,2:T(8,128)(2,1)} %get-tuple-element.415, s32[]{:T(128)} %get-tuple-element.402, pred[256,2048]{0,1:T(8,128)(4,1)S(1)} %dynamic-slice_bitcast_fusion.4), kind=kOutput, calls=%fused_computation.2.clone.1 | convolution fusion | flops 549452800 | bytes 6033920 | tf_op jit(solution)/shard_map/while/body/eval_jaxpr/tkgd,skd->kgts/dot_general | solution.py:34
  300.5 2.1 fusion.43
  302.9 4.3 %convert_reduce_fusion.4 = (f32[2,2,256]{2,1,0:T(2,128)S(1)}, bf16[2,2,256,2048]{2,3,1,0:T(8,128)(2,1)S(1)}) fusion(bf16[256,2,2,128]{3,0,2,1:T(8,128)(2,1)S(1)} %get-tuple-element.416, bf16[4,2048,2,128]{3,1,0,2:T(8,128)(2,1)} %get-tuple-element.415, s32[]{:T(128)} %get-tuple-element.402, pred[256,2048]{0,1:T(8,128)(4,1)S(1)} %dynamic-slice_bitcast_fusion.4), kind=kOutput, calls=%fused_computation.2.clone.1 | convolution fusion | flops 549452800 | bytes 6033920 | tf_op jit(solution)/shard_map/while/body/eval_jaxpr/tkgd,skd->kgts/dot_general | solution.py:34
  307.2 2.1 fusion.43
  309.8 5.2 %convolution_convert_fusion = bf16[256,4608]{1,0:T(8,128)(2,1)} fusion(bf16[256,512]{1,0:T(8,128)(2,1)S(1)} %bitcast.115, bf16[512,4608]{1,0:T(8,128)(2,1)} %bitcast.116), kind=kOutput, calls=%fused_computation.27 | convolution fusion | flops 1209139200 | bytes 7340032 | tf_op jit(solution)/shard_map/dot_general | solution.py:132
  315.0 81.9 %reduce-scatter.2.cloned.1.call-done = bf16[32,4608]{1,0:T(8,128)(2,1)} async-done(((bf16[256,4608]{1,0:T(8,128)(2,1)}), bf16[32,4608]{1,0:T(8,128)(2,1)}) %reduce-scatter.2.cloned.1.call-update) | async-done | bytes 294928 | tf_op jit(solution)/shard_map/reduce_scatter | solution.py:131
  398.1 1.8 add_convert_fusion
  (57 shorter events, 10.4 us)
Async XLA Ops:
  6.5 17.7 %copy-start.1 = (bf16[2,128,4,128]{3,2,1,0:T(4,128)(2,1)S(1)}, bf16[2,128,4,128]{3,2,1,0:T(4,128)(2,1)}, u32[]{:S(2)}) copy-start(bf16[2,128,4,128]{3,2,1,0:T(4,128)(2,1)} %param.14) | copy-start | bytes 786436
  6.5 71.2 %all-gather.7.cloned.1.call-start = ((), (), s32[]{:S(2)}) async-start(), calls=%async_computation.2 | async-start | bytes 4325376 | tf_op jit(solution)/shard_map/all_gather | solution.py:84
  8.2 138.1 %all-gather.5.cloned.1.call-start = ((), (), s32[]{:S(2)}) async-start(), calls=%async_computation.1 | async-start | bytes 4325376 | tf_op jit(solution)/shard_map/all_gather | solution.py:85
  9.8 204.8 %all-gather.9.cloned.1.call-start = ((), (), s32[]{:S(2)}) async-start(), calls=%async_computation.3 | async-start | bytes 4325376 | tf_op jit(solution)/shard_map/all_gather | solution.py:104
  11.5 271.2 %all-gather.11.cloned.1.call-start = ((), (), s32[]{:S(2)}) async-start(), calls=%async_computation.4 | async-start | bytes 4325376 | tf_op jit(solution)/shard_map/all_gather | solution.py:103
  13.1 383.8 %reduce-scatter.2.cloned.1.call-start = ((), (), s32[]{:S(2)}) async-start(), calls=%async_computation.5 | async-start | bytes 2654208 | tf_op jit(solution)/shard_map/reduce_scatter | solution.py:131
  309.8 88.4 %copy-start = (bf16[2,16,4608]{2,1,0:T(8,128)(2,1)S(1)}, bf16[2,16,4608]{2,1,0:T(8,128)(2,1)}, u32[]{:S(2)}) copy-start(bf16[2,16,4608]{2,1,0:T(8,128)(2,1)} %param.22) | copy-start | bytes 884740
  309.8 88.3 %copy-start.2 = (f32[4608]{0:T(1024)S(1)}, f32[4608]{0:T(1024)}, u32[]{:S(2)}) copy-start(f32[4608]{0:T(1024)} %param.23) | copy-start | bytes 55300
Sparse Core Ops, SparseCore 0:
  9.2 68.4 all-gather.6
  79.6 66.6 all-gather.4
  148.2 66.3 all-gather.8
  216.3 66.3 all-gather.10
  315.1 81.7 reduce-scatter.1
where the time goes:
time: 407 us; the launch traced here: 406 us
  waiting for transfers between devices  297 us (73%)
  matrix products  67.5 us (17%)
  local copies, waits for them, and re-layouts  17.6 us (4%)
  between operations  13.3 us (3%)
  other arithmetic  10.9 us (3%)
    reduce_scatter x1, waiting for transfers between devices, shards(): lax.psum_scatter(jnp.dot(attended, weight_rows, preferred_element_type=jn...  81.9 us
    all_gather x1, waiting for transfers between devices, shards(): lax.all_gather(pool_values, 'blk', axis=0, tiled=True)  68.5 us
    all_gather x1, waiting for transfers between devices, shards(): lax.all_gather(new_keys, 'blk', axis=1, tiled=True)  68.1 us
    all_gather x1, waiting for transfers between devices, shards(): lax.all_gather(pool_keys, 'blk', axis=0, tiled=True)  51.5 us
    dot_general x8, matrix products, compute(): jnp.einsum('tkgd,skd->kgts', grouped, key_block, preferred_element_type=j...  39.8 us
    all_gather x1, waiting for transfers between devices, shards(): lax.all_gather(new_values, 'blk', axis=1, tiled=True)  26.7 us
    dot_general x8, matrix products, compute(): jnp.einsum('kgts,skd->tkgd', weights, value_block, preferred_element_type...  22.4 us
  transfers between devices with their start and end apart: 5, of which 5 were waited for; matrix products, arithmetic and copies ran while one was open for 15% of the time, Pallas kernels for 0%

commit v1 on v0

--- a/solution.py
+++ b/solution.py
@@ -101,7 +101,9 @@
     )
     pieces = (
         lax.all_gather(new_keys, "blk", axis=1, tiled=True),
-        lax.all_gather(new_values, "blk", axis=1, tiled=True),
+        jnp.concatenate(
+            lax.all_to_all(jnp.stack([new_values] * lax.axis_size("blk")), "blk", 0, 0), axis=1
+        ),
     )
     piece_pages = pieces[0].shape[1] // page_len
     page_index = jnp.arange(req_count * piece_pages, dtype=jnp.int32)

time: 407 us -> 386 us (0.948)
  waiting for transfers between devices: 297 us -> 261 us
  starting transfers between devices: 0.17 us -> 9.97 us
  local copies, waits for them, and re-layouts: 17.6 us -> 23.7 us
    all_to_all x0 -> x1, waiting for transfers between devices: none -> 100 us  [shards(): lax.all_to_all(jnp.stack([new_values] * lax.axis_size('blk')), 'blk', 0, 0)]
    all_gather x1, waiting for transfers between devices: 51.5 us -> 0.01 us  [shards(): lax.all_gather(pool_keys, 'blk', axis=0, tiled=True)]
    all_gather x1, waiting for transfers between devices: 68.1 us -> 26.7 us  [shards(): lax.all_gather(new_keys, 'blk', axis=1, tiled=True)]
    all_gather x1 -> x0, waiting for transfers between devices: 26.7 us -> none  [shards(): lax.all_gather(new_values, 'blk', axis=1, tiled=True)]
    all_gather x1, waiting for transfers between devices: 68.5 us -> 52.2 us  [shards(): lax.all_gather(pool_values, 'blk', axis=0, tiled=True)]
    all_to_all x0 -> x1, starting transfers between devices: none -> 9.85 us  [shards(): lax.all_to_all(jnp.stack([new_values] * lax.axis_size('blk')), 'blk', 0, 0)]
    all_to_all x0 -> x1, local copies, waits for them, and re-layouts: none -> 4.74 us  [shards(): lax.all_to_all(jnp.stack([new_values] * lax.axis_size('blk')), 'blk', 0, 0)]
  transfers between devices with their start and end apart: 5 -> 5, of which waited for: 5 -> 4; matrix products, arithmetic and copies ran while one was open for 15% -> 16% of each run, Pallas kernels for 0% -> 0%
where the time goes in v1:
time: 386 us; the launch traced here: 385 us
  waiting for transfers between devices  261 us (68%)
  matrix products  67.6 us (18%)
  local copies, waits for them, and re-layouts  23.7 us (6%)
  between operations  13.3 us (3%)
  starting transfers between devices  9.97 us (3%)
  other arithmetic  8.87 us (2%)
    all_to_all x1, waiting for transfers between devices, shards(): lax.all_to_all(jnp.stack([new_values] * lax.axis_size('blk')), 'blk', 0, 0)  100 us
    reduce_scatter x1, waiting for transfers between devices, shards(): lax.psum_scatter(jnp.dot(attended, weight_rows, preferred_element_type=jn...  81.8 us
    all_gather x1, waiting for transfers between devices, shards(): lax.all_gather(pool_values, 'blk', axis=0, tiled=True)  52.2 us
    dot_general x8, matrix products, compute(): jnp.einsum('tkgd,skd->kgts', grouped, key_block, preferred_element_type=j...  39.9 us
    all_gather x1, waiting for transfers between devices, shards(): lax.all_gather(new_keys, 'blk', axis=1, tiled=True)  26.7 us
    dot_general x8, matrix products, compute(): jnp.einsum('kgts,skd->tkgd', weights, value_block, preferred_element_type...  22.4 us
    all_to_all x1, starting transfers between devices, shards(): lax.all_to_all(jnp.stack([new_values] * lax.axis_size('blk')), 'blk', 0, 0)  9.85 us
  transfers between devices with their start and end apart: 5, of which 4 were waited for; matrix products, arithmetic and copies ran while one was open for 16% of the time, Pallas kernels for 0%

profile of v1, /device:TPU:32, one launch (start us, length us, event | category | flops | bytes accessed | tf_op | source)
XLA Modules:
  0.0 384.5 jit_solution(17649202417222002196)
XLA Ops:
  6.5 1.6 copy.47
  8.2 1.6 copy.43
  10.7 3.0 stack.2
  13.7 9.8 %all-to-all-start = ((bf16[32,2,128,2,128]{4,2,1,3,0:T(8,128)(2,1)}), bf16[32,2,128,2,128]{4,2,1,3,0:T(8,128)(2,1)}, u32[]{:S(2)}, u32[]{:S(2)}) async-start(bf16[32,2,128,2,128]{4,2,1,3,0:T(8,128)(2,1)} %stack.2), calls=%async_computation | async-start | bytes 8388608 | tf_op jit(solution)/shard_map/all_to_all | solution.py:105
  25.1 3.5 and_reduce_fusion
  28.6 4.8 %copy.46 = pred[4,256,16,128]{1,3,2,0:T(8,128)(4,1)} copy(pred[4,256,16,128]{3,1,2,0:T(8,128)(4,1)S(1)} %bitcast.111) | data formatting | bytes 4194304 | tf_op jit(solution)/shard_map/transpose | solution.py:27
  33.7 1.7 bitcast_and_fusion
  35.4 100.0 %all-to-all-done = bf16[32,2,128,2,128]{4,2,1,3,0:T(8,128)(2,1)} async-done(((bf16[32,2,128,2,128]{4,2,1,3,0:T(8,128)(2,1)}), bf16[32,2,128,2,128]{4,2,1,3,0:T(8,128)(2,1)}, u32[]{:S(2)}, u32[]{:S(2)}) %all-to-all-start) | async-done | bytes 4194336 | tf_op jit(solution)/shard_map/all_to_all | solution.py:105
  135.5 4.7 %copy.52 = bf16[32,2,128,2,128]{4,2,0,1,3:T(8,128)(2,1)} copy(bf16[32,2,128,2,128]{4,2,1,3,0:T(8,128)(2,1)} %all-to-all-done) | data formatting | bytes 8388608 | tf_op jit(solution)/shard_map/all_to_all | solution.py:105
  140.2 52.2 %all-gather.4.cloned.1.call-done = bf16[64,128,2,128]{3,1,0,2:T(8,128)(2,1)} async-done(((bf16[2,128,2,128]{3,1,0,2:T(8,128)(2,1)}), bf16[64,128,2,128]{3,1,0,2:T(8,128)(2,1)}) %all-gather.4.cloned.1.call-update) | async-done | bytes 4194320 | tf_op jit(solution)/shard_map/all_gather | solution.py:85
  192.5 41.6 %while.30 = (s32[]{:T(128)}, f32[256,2,2,128]{0,3,2,1:T(8,128)S(1)}, f32[2,2,256]{2,1,0:T(2,128)S(1)}, bf16[4,2048,2,128]{3,1,0,2:T(8,128)(2,1)}, pred[4,256,204...) while((s32[]{:T(128)}, ...), condition=%wide.region_5.6_spmd.clone, body=%wide.region_3.5_spmd.clone.sunk | while | flops 1086587904 | bytes 13386860 | solution.py:50
  193.7 5.7 %convert_reduce_fusion.5 = (f32[2,2,256]{2,1,0:T(2,128)S(1)}, bf16[2,2,256,2048]{2,3,1,0:T(8,128)(2,1)}) fusion(bf16[256,2,2,128]{3,0,2,1:T(8,128)(2,1)S(1)} %get-tuple-element.405, bf16[4,2048,2,128]{3,1,0,2:T(8,128)(2,1)} %get-tuple-element.404, s32[]{:T(128)} %get-tuple-element.390, pred[256,2048]{0,1:T(8,128)(4,1)S(1)} %dynamic-slice_bitcast_fusion.5), kind=kOutput, calls=%fused_computation.14.clone.1 | convolution fusion | flops 549452800 | bytes 6033920 | tf_op jit(solution)/shard_map/while/body/eval_jaxpr/tkgd,skd->kgts/dot_general | solution.py:34
  199.4 3.4 fusion.47
  204.1 5.7 %convert_reduce_fusion.5 = (f32[2,2,256]{2,1,0:T(2,128)S(1)}, bf16[2,2,256,2048]{2,3,1,0:T(8,128)(2,1)}) fusion(bf16[256,2,2,128]{3,0,2,1:T(8,128)(2,1)S(1)} %get-tuple-element.405, bf16[4,2048,2,128]{3,1,0,2:T(8,128)(2,1)} %get-tuple-element.404, s32[]{:T(128)} %get-tuple-element.390, pred[256,2048]{0,1:T(8,128)(4,1)S(1)} %dynamic-slice_bitcast_fusion.5), kind=kOutput, calls=%fused_computation.14.clone.1 | convolution fusion | flops 549452800 | bytes 6033920 | tf_op jit(solution)/shard_map/while/body/eval_jaxpr/tkgd,skd->kgts/dot_general | solution.py:34
  209.7 3.5 fusion.47
  214.5 5.7 %convert_reduce_fusion.5 = (f32[2,2,256]{2,1,0:T(2,128)S(1)}, bf16[2,2,256,2048]{2,3,1,0:T(8,128)(2,1)}) fusion(bf16[256,2,2,128]{3,0,2,1:T(8,128)(2,1)S(1)} %get-tuple-element.405, bf16[4,2048,2,128]{3,1,0,2:T(8,128)(2,1)} %get-tuple-element.404, s32[]{:T(128)} %get-tuple-element.390, pred[256,2048]{0,1:T(8,128)(4,1)S(1)} %dynamic-slice_bitcast_fusion.5), kind=kOutput, calls=%fused_computation.14.clone.1 | convolution fusion | flops 549452800 | bytes 6033920 | tf_op jit(solution)/shard_map/while/body/eval_jaxpr/tkgd,skd->kgts/dot_general | solution.py:34
  220.2 3.5 fusion.47
  225.0 5.7 %convert_reduce_fusion.5 = (f32[2,2,256]{2,1,0:T(2,128)S(1)}, bf16[2,2,256,2048]{2,3,1,0:T(8,128)(2,1)}) fusion(bf16[256,2,2,128]{3,0,2,1:T(8,128)(2,1)S(1)} %get-tuple-element.405, bf16[4,2048,2,128]{3,1,0,2:T(8,128)(2,1)} %get-tuple-element.404, s32[]{:T(128)} %get-tuple-element.390, pred[256,2048]{0,1:T(8,128)(4,1)S(1)} %dynamic-slice_bitcast_fusion.5), kind=kOutput, calls=%fused_computation.14.clone.1 | convolution fusion | flops 549452800 | bytes 6033920 | tf_op jit(solution)/shard_map/while/body/eval_jaxpr/tkgd,skd->kgts/dot_general | solution.py:34
  230.6 3.4 fusion.47
  234.1 26.7 %all-gather.8.cloned.1.call-done = bf16[2,4096,2,128]{3,1,0,2:T(8,128)(2,1)} async-done(((bf16[2,128,2,128]{3,1,0,2:T(8,128)(2,1)}), bf16[2,4096,2,128]{3,1,0,2:T(8,128)(2,1)}) %all-gather.8.cloned.1.call-update) | async-done | bytes 4194320 | tf_op jit(solution)/shard_map/all_gather | solution.py:103
  260.8 26.7 %while.29 = (s32[]{:T(128)}, f32[256,2,2,128]{0,3,2,1:T(8,128)S(1)}, f32[2,2,256]{2,1,0:T(2,128)S(1)}, bf16[4,2048,2,128]{3,1,0,2:T(8,128)(2,1)}, pred[4,256,204...) while((s32[]{:T(128)}, ...), condition=%wide.region_8.9_spmd, body=%wide.region_6.8_spmd.sunk | while | flops 1086455808 | bytes 13386841 | solution.py:50
  261.0 4.3 %convert_reduce_fusion.4 = (f32[2,2,256]{2,1,0:T(2,128)S(1)}, bf16[2,2,256,2048]{2,3,1,0:T(8,128)(2,1)S(1)}) fusion(bf16[256,2,2,128]{3,0,2,1:T(8,128)(2,1)S(1)} %get-tuple-element.430, bf16[4,2048,2,128]{3,1,0,2:T(8,128)(2,1)} %get-tuple-element.429, s32[]{:T(128)} %get-tuple-element.416, pred[256,2048]{0,1:T(8,128)(4,1)S(1)} %dynamic-slice_bitcast_fusion.4), kind=kOutput, calls=%fused_computation.2.clone.1 | convolution fusion | flops 549452800 | bytes 6033920 | tf_op jit(solution)/shard_map/while/body/eval_jaxpr/tkgd,skd->kgts/dot_general | solution.py:34
  265.3 2.1 fusion.43
  267.6 4.3 %convert_reduce_fusion.4 = (f32[2,2,256]{2,1,0:T(2,128)S(1)}, bf16[2,2,256,2048]{2,3,1,0:T(8,128)(2,1)S(1)}) fusion(bf16[256,2,2,128]{3,0,2,1:T(8,128)(2,1)S(1)} %get-tuple-element.430, bf16[4,2048,2,128]{3,1,0,2:T(8,128)(2,1)} %get-tuple-element.429, s32[]{:T(128)} %get-tuple-element.416, pred[256,2048]{0,1:T(8,128)(4,1)S(1)} %dynamic-slice_bitcast_fusion.4), kind=kOutput, calls=%fused_computation.2.clone.1 | convolution fusion | flops 549452800 | bytes 6033920 | tf_op jit(solution)/shard_map/while/body/eval_jaxpr/tkgd,skd->kgts/dot_general | solution.py:34
  272.0 2.1 fusion.43
  274.3 4.3 %convert_reduce_fusion.4 = (f32[2,2,256]{2,1,0:T(2,128)S(1)}, bf16[2,2,256,2048]{2,3,1,0:T(8,128)(2,1)S(1)}) fusion(bf16[256,2,2,128]{3,0,2,1:T(8,128)(2,1)S(1)} %get-tuple-element.430, bf16[4,2048,2,128]{3,1,0,2:T(8,128)(2,1)} %get-tuple-element.429, s32[]{:T(128)} %get-tuple-element.416, pred[256,2048]{0,1:T(8,128)(4,1)S(1)} %dynamic-slice_bitcast_fusion.4), kind=kOutput, calls=%fused_computation.2.clone.1 | convolution fusion | flops 549452800 | bytes 6033920 | tf_op jit(solution)/shard_map/while/body/eval_jaxpr/tkgd,skd->kgts/dot_general | solution.py:34
  278.6 2.1 fusion.43
  281.0 4.3 %convert_reduce_fusion.4 = (f32[2,2,256]{2,1,0:T(2,128)S(1)}, bf16[2,2,256,2048]{2,3,1,0:T(8,128)(2,1)S(1)}) fusion(bf16[256,2,2,128]{3,0,2,1:T(8,128)(2,1)S(1)} %get-tuple-element.430, bf16[4,2048,2,128]{3,1,0,2:T(8,128)(2,1)} %get-tuple-element.429, s32[]{:T(128)} %get-tuple-element.416, pred[256,2048]{0,1:T(8,128)(4,1)S(1)} %dynamic-slice_bitcast_fusion.4), kind=kOutput, calls=%fused_computation.2.clone.1 | convolution fusion | flops 549452800 | bytes 6033920 | tf_op jit(solution)/shard_map/while/body/eval_jaxpr/tkgd,skd->kgts/dot_general | solution.py:34
  285.3 2.1 fusion.43
  287.9 5.2 %convolution_convert_fusion = bf16[256,4608]{1,0:T(8,128)(2,1)} fusion(bf16[256,512]{1,0:T(8,128)(2,1)S(1)} %bitcast.117, bf16[512,4608]{1,0:T(8,128)(2,1)} %bitcast.118), kind=kOutput, calls=%fused_computation.27 | convolution fusion | flops 1209139200 | bytes 7340032 | tf_op jit(solution)/shard_map/dot_general | solution.py:134
  293.1 81.8 %reduce-scatter.2.cloned.1.call-done = bf16[32,4608]{1,0:T(8,128)(2,1)} async-done(((bf16[256,4608]{1,0:T(8,128)(2,1)}), bf16[32,4608]{1,0:T(8,128)(2,1)}) %reduce-scatter.2.cloned.1.call-update) | async-done | bytes 294928 | tf_op jit(solution)/shard_map/reduce_scatter | solution.py:133
  376.2 1.8 add_convert_fusion
  (64 shorter events, 10.0 us)
Async XLA Ops:
  6.5 133.7 %all-gather.6.cloned.1.call-start = ((), (), s32[]{:S(2)}) async-start(), calls=%async_computation.3 | async-start | bytes 4325376 | tf_op jit(solution)/shard_map/all_gather | solution.py:84
  8.1 184.3 %all-gather.4.cloned.1.call-start = ((), (), s32[]{:S(2)}) async-start(), calls=%async_computation.2 | async-start | bytes 4325376 | tf_op jit(solution)/shard_map/all_gather | solution.py:85
  13.7 9.9 %copy-start.2 = (bf16[2,128,2,128]{3,2,1,0:T(2,128)(2,1)S(1)}, bf16[2,128,2,128]{3,2,1,0:T(2,128)(2,1)}, u32[]{:S(2)}) copy-start(bf16[2,128,2,128]{3,2,1,0:T(2,128)(2,1)} %param.15) | copy-start | bytes 393220
  13.7 10.7 %copy-start.4 = (s32[2,32]{1,0:T(2,128)S(1)}, s32[2,32]{1,0:T(2,128)}, u32[]{:S(2)}) copy-start(s32[2,32]{1,0:T(2,128)} %param.19) | copy-start | bytes 772
  13.7 11.1 %copy-start.5 = (s32[2]{0:T(128)S(1)}, s32[2]{0:T(128)}, u32[]{:S(2)}) copy-start(s32[2]{0:T(128)} %param.20) | copy-start | bytes 28
  13.7 121.7 %all-to-all-start = ((bf16[32,2,128,2,128]{4,2,1,3,0:T(8,128)(2,1)}), bf16[32,2,128,2,128]{4,2,1,3,0:T(8,128)(2,1)}, u32[]{:S(2)}, u32[]{:S(2)}) async-start(bf16[32,2,128,2,128]{4,2,1,3,0:T(8,128)(2,1)} %stack.2), calls=%async_computation | async-start | bytes 8388608 | tf_op jit(solution)/shard_map/all_to_all | solution.py:105
  23.6 9.8 %copy-start.1 = (bf16[2,128,4,128]{3,2,1,0:T(4,128)(2,1)S(1)}, bf16[2,128,4,128]{3,2,1,0:T(4,128)(2,1)}, u32[]{:S(2)}) copy-start(bf16[2,128,4,128]{3,2,1,0:T(4,128)(2,1)} %param.14) | copy-start | bytes 786436
  23.6 237.2 %all-gather.8.cloned.1.call-start = ((), (), s32[]{:S(2)}) async-start(), calls=%async_computation.4 | async-start | bytes 4325376 | tf_op jit(solution)/shard_map/all_gather | solution.py:103
  24.3 350.6 %reduce-scatter.2.cloned.1.call-start = ((), (), s32[]{:S(2)}) async-start(), calls=%async_computation.5 | async-start | bytes 2654208 | tf_op jit(solution)/shard_map/reduce_scatter | solution.py:133
  287.9 88.3 %copy-start = (bf16[2,16,4608]{2,1,0:T(8,128)(2,1)S(1)}, bf16[2,16,4608]{2,1,0:T(8,128)(2,1)}, u32[]{:S(2)}) copy-start(bf16[2,16,4608]{2,1,0:T(8,128)(2,1)} %param.22) | copy-start | bytes 884740
  287.9 88.3 %copy-start.3 = (f32[4608]{0:T(1024)S(1)}, f32[4608]{0:T(1024)}, u32[]{:S(2)}) copy-start(f32[4608]{0:T(1024)} %param.23) | copy-start | bytes 55300
Sparse Core Ops, SparseCore 0:
  9.2 109.6 all-gather.5
  120.8 71.6 all-gather.3
  194.3 66.3 all-gather.7
  293.2 81.6 reduce-scatter.1
